TPU v7x, 512 devices: a whole 4x8x8 slice. The times are simulated.
512 devices in a mesh: ctx: 16 (over z_hi, x), tp: 8 (over y), dp: 4 (over z_lo, core).
Axes of the slice: x: 4, y: 8, z: 8 (z_hi: 4, z_lo: 2; z = z_hi * 2 + z_lo), core: 2. Of those that a mesh axis runs over, the one named last changes fastest.
Arguments:
- q_raw: bfloat16 [4, 2048, 2048], P('dp', 'ctx', 'tp'), may hold values from -60 to 60
- k_raw: bfloat16 [4, 2048, 2048], P('dp', 'ctx', 'tp'), may hold values from -60 to 60
- value: bfloat16 [4, 2048, 2048], P('dp', 'ctx', 'tp'), may hold values from -6 to 6
- d_out: bfloat16 [4, 2048, 2048], P('dp', 'ctx', 'tp'), may hold values from -6 to 6
- q_gain: float32 [128], replicated, may hold values from 1.3 to 5
- k_gain: float32 [128], replicated, may hold values from 1.3 to 5
Outputs:
- q_raw_grad: bfloat16 [4, 2048, 2048], P('dp', 'ctx', 'tp')
- k_raw_grad: bfloat16 [4, 2048, 2048], P('dp', 'ctx', 'tp')
- value_grad: bfloat16 [4, 2048, 2048], P('dp', 'ctx', 'tp')
- q_gain_grad: float32 [128], replicated
- k_gain_grad: float32 [128], replicated
All inputs are finite; a program needn't handle non-finite values.
Results may differ from a plain program's by a relative error of at most 0.028.
The roundings to bfloat16 on the way count: a program that leaves them out, or rounds other values in their place, can miss the bound.
Values may be sent and summed in bfloat16 or wider, within the bound.
A program may use at most 64 MiB of HBM per device.

v0:
```python
import math
import jax
import jax.numpy as jnp
from jax import lax
from jax.sharding import PartitionSpec as P

EPSILON = 1e-06


def normalize(raw, gain, heads_here):
    rows = raw.shape[0]
    width = gain.shape[0]
    values = raw.astype(jnp.float32).reshape(rows, heads_here, width)
    inverse = lax.rsqrt(jnp.mean(values * values, axis=2, keepdims=True) + EPSILON)
    unit = values * inverse
    return (unit, inverse, (unit * gain).astype(jnp.bfloat16))


def restore(grad_normed, unit, inverse, gain):
    scaled = grad_normed * gain
    back = inverse * (scaled - unit * jnp.mean(scaled * unit, axis=2, keepdims=True))
    return (back, jnp.sum(grad_normed * unit, axis=(0, 1)))


def block_weights(query_normed, query_out, log_total, delta, key_normed, key_value_pair, scale):
    scores = (
        jnp.einsum("qhd,khd->hqk", query_normed, key_normed, preferred_element_type=jnp.float32)
        * scale
    )
    prob = jnp.exp(scores - log_total[:, :, None])
    dprob = jnp.einsum(
        "qhd,khd->hqk", query_out, key_value_pair, preferred_element_type=jnp.float32
    )
    prob_low = prob.astype(jnp.bfloat16)
    dscore = (prob * (dprob - delta[:, :, None]) * scale).astype(jnp.bfloat16)
    return (prob_low, dscore)


def key_block_terms(query_normed, query_out, log_total, delta, key_normed, key_value_pair, scale):
    prob_low, dscore = block_weights(
        query_normed, query_out, log_total, delta, key_normed, key_value_pair, scale
    )
    dkey = jnp.einsum("hqk,qhd->khd", dscore, query_normed, preferred_element_type=jnp.float32)
    dval = jnp.einsum("hqk,qhd->khd", prob_low, query_out, preferred_element_type=jnp.float32)
    return (dkey, dval)


def local(q_raw, k_raw, value, d_out, q_gain, k_gain):
    width = q_gain.shape[0]
    rows = q_raw.shape[1]
    heads_here = q_raw.shape[2] // width
    flat = heads_here * width
    scale = width ** (-0.5)
    q_unit, q_inverse, q_normed = normalize(q_raw[0], q_gain, heads_here)
    k_unit, k_inverse, k_normed = normalize(k_raw[0], k_gain, heads_here)
    own_value = value[0]
    own_out_flat = d_out[0]
    own_out = own_out_flat.reshape(rows, heads_here, width)
    all_keys, all_values = (
        lax.all_gather(k_normed.reshape(rows, flat), "ctx", axis=0, tiled=True),
        lax.all_gather(own_value, "ctx", axis=0, tiled=True),
    )
    length = all_keys.shape[0]
    block = min(512, length)
    block_count = length // block

    def key_slice(begin, size):
        keys = lax.dynamic_slice_in_dim(all_keys, begin, size, 0).reshape(size, heads_here, width)
        vals = lax.dynamic_slice_in_dim(all_values, begin, size, 0).reshape(size, heads_here, width)
        return (keys, vals)

    def statistics(index, carry):
        top, total, weighted = carry
        keys, vals = key_slice(index * block, block)
        scores = (
            jnp.einsum("qhd,khd->hqk", q_normed, keys, preferred_element_type=jnp.float32) * scale
        )
        dprob = jnp.einsum("qhd,khd->hqk", own_out, vals, preferred_element_type=jnp.float32)
        new_top = jnp.maximum(top, jnp.max(scores, axis=2))
        factor = jnp.exp(top - new_top)
        expo = jnp.exp(scores - new_top[:, :, None])
        return (
            new_top,
            total * factor + jnp.sum(expo, axis=2),
            weighted * factor + jnp.sum(expo * dprob, axis=2),
        )

    start_top = jnp.full((heads_here, rows), -jnp.inf, jnp.float32)
    zero_stat = jnp.zeros((heads_here, rows), jnp.float32)
    top, total, weighted = lax.fori_loop(
        0, block_count, statistics, (start_top, zero_stat, zero_stat)
    )
    log_total = top + jnp.log(total)
    delta = weighted / total

    def query_pass(index, acc):
        keys, vals = key_slice(index * block, block)
        prob_low, dscore = block_weights(q_normed, own_out, log_total, delta, keys, vals, scale)
        return acc + jnp.einsum("hqk,khd->qhd", dscore, keys, preferred_element_type=jnp.float32)

    dq_normed = lax.fori_loop(
        0, block_count, query_pass, jnp.zeros((rows, heads_here, width), jnp.float32)
    )
    dq_back, q_gain_part = restore(dq_normed, q_unit, q_inverse, q_gain)
    size = math.gcd(lax.axis_size("ctx") * rows, 512)

    def one_block(index):
        keys, vals = key_slice(index * size, size)
        dkey, dval = key_block_terms(q_normed, own_out, log_total, delta, keys, vals, scale)
        return jnp.concatenate([dkey.reshape(size, flat), dval.reshape(size, flat)], axis=1)

    summed = lax.psum_scatter(
        lax.map(one_block, jnp.arange(lax.axis_size("ctx") * rows // size))
        .reshape(lax.axis_size("ctx") * rows, 2 * flat)
        .astype(jnp.bfloat16),
        "ctx",
        scatter_dimension=0,
        tiled=True,
    ).astype(jnp.float32)
    dk_normed = summed[:, :flat]
    dv_sum = summed[:, flat:]
    dk_back, k_gain_part = restore(
        dk_normed.reshape(rows, heads_here, width), k_unit, k_inverse, k_gain
    )
    q_gain_total, k_gain_total = lax.psum((q_gain_part, k_gain_part), ("ctx", "tp", "dp"))
    q_grad = dq_back.reshape(rows, flat).astype(jnp.bfloat16)[None]
    k_grad = dk_back.reshape(rows, flat).astype(jnp.bfloat16)[None]
    value_grad = dv_sum.astype(jnp.bfloat16)[None]
    return (q_grad, k_grad, value_grad, q_gain_total / length, k_gain_total / length)


def solution(mesh):
    return jax.shard_map(
        local,
        mesh=mesh,
        in_specs=(
            P("dp", "ctx", "tp"),
            P("dp", "ctx", "tp"),
            P("dp", "ctx", "tp"),
            P("dp", "ctx", "tp"),
            P(),
            P(),
        ),
        out_specs=(P("dp", "ctx", "tp"), P("dp", "ctx", "tp"), P("dp", "ctx", "tp"), P(), P()),
        check_vma=False,
    )
```

profile of v0, /device:TPU:1, one launch (start us, length us, event | category | flops | bytes accessed | tf_op | source)
XLA Modules:
  0.0 363.0 jit_solution(17884126247453620999)
XLA Ops:
  7.2 0.7 broadcast_bitcast_fusion
  7.9 0.9 reshape.126
  9.2 1.5 multiply_convert_fusion.2
  10.8 1.6 copy.113
  12.5 1.0 copy.114
  13.6 0.9 copy.110
  14.6 0.7 multiply_convert_fusion.1
  15.4 59.9 %all-gather.4.cloned.1.call-done = bf16[2048,256]{1,0:T(8,128)(2,1)} async-done(((bf16[128,256]{1,0:T(8,128)(2,1)}), bf16[2048,256]{1,0:T(8,128)(2,1)}) %all-gather.4.cloned.1.call-update) | async-done | bytes 1048592 | tf_op jit(solution)/shard_map/all_gather | solution.py:60
  75.4 1.5 copy.118
  76.9 60.4 %all-gather.6.cloned.1.call-done = bf16[1,2048,256]{1,2,0:T(8,128)(2,1)} async-done(((bf16[1,128,256]{1,2,0:T(8,128)(2,1)}), bf16[1,2048,256]{1,2,0:T(8,128)(2,1)}) %all-gather.6.cloned.1.call-update) | async-done | bytes 1048592 | tf_op jit(solution)/shard_map/all_gather | solution.py:61
  137.3 7.0 %while.43 = (s32[]{:T(128)}, f32[2,128]{1,0:T(2,128)S(1)}, f32[2,128]{1,0:T(2,128)S(1)}, f32[2,128]{1,0:T(2,128)S(1)}, bf16[2048,256]{0,1:T(8,128)(2,1)S(1)}, /*...) while((s32[]{:T(128)}, f32[2,128]{1,0:T(2,128)S(1)}, ...), condition=%wide.region_6.0_spmd.clone, body=%wide.region_2.0_spmd.clone.sunk | while | flops 68028160 | bytes 3295418 | solution.py:90
  137.3 1.0 constant_dynamic-slice_fusion.10
  139.0 1.0 constant_dynamic-slice_fusion.10
  140.8 1.0 constant_dynamic-slice_fusion.10
  142.6 1.0 constant_dynamic-slice_fusion.10
  144.3 16.4 %while.42 = (s32[]{:T(128)}, bf16[4,512,512]{1,2,0:T(8,128)(2,1)}, s32[4]{0:T(128)S(1)}, bf16[2048,256]{0,1:T(8,128)(2,1)S(1)}, bf16[128,2,128]{0,2,1:T(8,128)(2...) while((s32[]{:T(128)}, bf16[4,512,512]{1,2,0:T(8,128)(2,1)}, ...), condition=%wide.region_11.12_spmd, body=%wide.region_10.0_spmd.sunk | while | flops 136183808 | bytes 4982983 | solution.py:113
  144.3 0.6 dynamic_slice.53
  145.6 1.0 constant_dynamic-slice_fusion.9
  146.9 0.5 fusion.87
  147.6 0.8 fusion.88
  148.4 0.6 dynamic_slice.53
  149.7 1.0 constant_dynamic-slice_fusion.9
  151.0 0.5 fusion.87
  151.7 0.9 fusion.88
  152.6 0.6 dynamic_slice.53
  153.8 1.0 constant_dynamic-slice_fusion.9
  155.1 0.5 fusion.87
  155.8 0.8 fusion.88
  156.6 0.6 dynamic_slice.53
  157.9 1.0 constant_dynamic-slice_fusion.9
  159.2 0.5 fusion.87
  159.9 0.9 fusion.88
  160.8 4.1 %copy.123 = bf16[4,512,512]{2,1,0:T(8,128)(2,1)} copy(bf16[4,512,512]{1,2,0:T(8,128)(2,1)} %get-tuple-element.336) | data formatting | bytes 4194304 | tf_op jit(solution)/shard_map/convert_element_type | solution.py:115
  165.0 7.3 %while.44 = (s32[]{:T(128)}, f32[128,2,128]{0,2,1:T(8,128)S(1)}, bf16[2048,256]{0,1:T(8,128)(2,1)S(1)}, bf16[128,2,128]{2,0,1:T(8,128)(2,1)S(1)}, f32[2,128]{1,0...) while((s32[]{:T(128)}, f32[128,2,128]{0,2,1:T(8,128)S(1)}, ...), condition=%wide.region_8.0_spmd.clone, body=%wide.region_7.0_spmd.clone.sunk | while | flops 101515264 | bytes 3279033 | solution.py:101
  165.0 1.0 constant_dynamic-slice_fusion.11
  166.3 0.5 fusion.104
  166.8 1.0 constant_dynamic-slice_fusion.11
  168.1 0.5 fusion.104
  168.7 1.0 constant_dynamic-slice_fusion.11
  170.0 0.5 fusion.104
  170.5 1.0 constant_dynamic-slice_fusion.11
  171.8 0.5 fusion.104
  172.5 0.7 copy.134
  173.3 82.7 %reduce-scatter.2.cloned.1.call-done = bf16[128,512]{1,0:T(8,128)(2,1)} async-done(((bf16[2048,512]{1,0:T(8,128)(2,1)}), bf16[128,512]{1,0:T(8,128)(2,1)}) %reduce-scatter.2.cloned.1.call-update) | async-done | bytes 131088 | tf_op jit(solution)/shard_map/reduce_scatter | solution.py:112
  255.9 1.5 slice_bitcast_fusion
  258.1 1.5 multiply_reduce_fusion
  259.7 96.3 %all-reduce = (f32[128]{0:T(128)S(1)}, f32[128]{0:T(128)S(1)}) all-reduce(f32[128]{0:T(128)S(1)} %get-tuple-element.541, f32[128]{0:T(128)S(1)} %bitcast_reduce_fusion), channel_id=1, replica_groups=mesh['ctx'=16,'tp'=8,'dp'=4] {'ctx','tp','dp'}, use_global_device_ids=true, to_apply=%region_15.16 | all-reduce | flops 256 | bytes 2048 | tf_op jit(solution)/shard_map/psum | solution.py:125
  355.9 0.5 broadcast_multiply_fusion.2
  (70 shorter events, 7.9 us)
Async XLA Ops:
  7.2 68.2 %all-gather.4.cloned.1.call-start = ((), (), s32[]{:S(2)}) async-start(), calls=%async_computation.1 | async-start | bytes 1114112 | tf_op jit(solution)/shard_map/all_gather | solution.py:60
  10.7 126.5 %all-gather.6.cloned.1.call-start = ((), (), s32[]{:S(2)}) async-start(), calls=%async_computation.3 | async-start | bytes 1114112 | tf_op jit(solution)/shard_map/all_gather | solution.py:61
  12.4 243.6 %reduce-scatter.2.cloned.1.call-start = ((), (), s32[]{:S(2)}) async-start(), calls=%async_computation.2 | async-start | bytes 2228224 | tf_op jit(solution)/shard_map/reduce_scatter | solution.py:112
  164.9 7.3 %copy-start.1 = (f32[128]{0:T(128)S(1)}, f32[128]{0:T(128)}, u32[]{:S(2)}) copy-start(f32[128]{0:T(128)} %param.16) | copy-start | bytes 1540
  165.0 92.6 %copy-start.2 = (f32[128]{0:T(128)S(1)}, f32[128]{0:T(128)}, u32[]{:S(2)}) copy-start(f32[128]{0:T(128)} %param.17) | copy-start | bytes 1540
  165.0 93.2 %copy-start = (bf16[1,128,256]{2,1,0:T(8,128)(2,1)S(1)}, bf16[1,128,256]{2,1,0:T(8,128)(2,1)}, u32[]{:S(2)}) copy-start(bf16[1,128,256]{2,1,0:T(8,128)(2,1)} %param.13) | copy-start | bytes 196612
Sparse Core Ops, SparseCore 0:
  11.6 63.7 all-gather.3
  78.9 58.3 all-gather.5
  165.1 90.8 reduce-scatter.1
where the time goes:
time: 364 us; the launch traced here: 363 us
  waiting for transfers between devices  203 us (56%)
  blocking collectives  96.3 us (26%)
  local copies, waits for them, and re-layouts  26.5 us (7%)
  between operations  14 us (4%)
  other arithmetic  10.5 us (3%)
  matrix products  9.47 us (3%)
    psum x1, blocking collectives, local(): lax.psum((q_gain_part, k_gain_part), ('ctx', 'tp', 'dp'))  96.3 us
    reduce_scatter x1, waiting for transfers between devices, local(): lax.psum_scatter(lax.map(one_block, jnp.arange(lax.axis_size('ctx') * row...  82.7 us
    all_gather x1, waiting for transfers between devices, local(): lax.all_gather(own_value, 'ctx', axis=0, tiled=True)  60.4 us
    all_gather x1, waiting for transfers between devices, local(): lax.all_gather(k_normed.reshape(rows, flat), 'ctx', axis=0, tiled=True)  59.9 us
    dynamic_slice x12, local copies, waits for them, and re-layouts, key_slice(): lax.dynamic_slice_in_dim(all_values, begin, size, 0)  12 us
  transfers between devices with their start and end apart: 3, of which 3 were waited for; matrix products, arithmetic and copies ran while one was open for 4% of the time, Pallas kernels for 0%

commit v1 on v0

--- a/solution.py
+++ b/solution.py
@@ -57,7 +57,12 @@
     own_out_flat = d_out[0]
     own_out = own_out_flat.reshape(rows, heads_here, width)
     all_keys, all_values = (
-        lax.all_gather(k_normed.reshape(rows, flat), "ctx", axis=0, tiled=True),
+        jnp.concatenate(
+            lax.all_to_all(
+                jnp.stack([k_normed.reshape(rows, flat)] * lax.axis_size("ctx")), "ctx", 0, 0
+            ),
+            axis=0,
+        ),
         lax.all_gather(own_value, "ctx", axis=0, tiled=True),
     )
     length = all_keys.shape[0]

time: 364 us -> 319 us (0.88)
  waiting for transfers between devices: 203 us -> 148 us
  starting transfers between devices: 0.12 us -> 13.5 us
    all_gather x1 -> x0, waiting for transfers between devices: 59.9 us -> none  [local(): lax.all_gather(k_normed.reshape(rows, flat), 'ctx', axis=0, tiled=True)]
    all_to_all x0 -> x1, waiting for transfers between devices: none -> 20.2 us  [local(): lax.all_to_all(jnp.stack([k_normed.reshape(rows, flat)] * lax.axis_size('...]
    all_gather x1, waiting for transfers between devices: 60.4 us -> 44.7 us  [local(): lax.all_gather(own_value, 'ctx', axis=0, tiled=True)]
    all_to_all x0 -> x1, starting transfers between devices: none -> 13.4 us  [local(): lax.all_to_all(jnp.stack([k_normed.reshape(rows, flat)] * lax.axis_size('...]
  transfers between devices with their start and end apart: 3 -> 3, of which waited for: 3 -> 3; matrix products, arithmetic and copies ran while one was open for 4% -> 3% of each run, Pallas kernels for 0% -> 0%
where the time goes in v1:
time: 319 us; the launch traced here: 318 us
  waiting for transfers between devices  148 us (46%)
  blocking collectives  96.2 us (30%)
  local copies, waits for them, and re-layouts  25.1 us (8%)
  between operations  14.3 us (4%)
  starting transfers between devices  13.5 us (4%)
  matrix products  9.48 us (3%)
  other arithmetic  9.27 us (3%)
    psum x1, blocking collectives, local(): lax.psum((q_gain_part, k_gain_part), ('ctx', 'tp', 'dp'))  96.2 us
    reduce_scatter x1, waiting for transfers between devices, local(): lax.psum_scatter(lax.map(one_block, jnp.arange(lax.axis_size('ctx') * row...  82.5 us
    all_gather x1, waiting for transfers between devices, local(): lax.all_gather(own_value, 'ctx', axis=0, tiled=True)  44.7 us
    all_to_all x1, waiting for transfers between devices, local(): lax.all_to_all(jnp.stack([k_normed.reshape(rows, flat)] * lax.axis_size('...  20.2 us
    all_to_all x1, starting transfers between devices, local(): lax.all_to_all(jnp.stack([k_normed.reshape(rows, flat)] * lax.axis_size('...  13.4 us
    dynamic_slice x12, local copies, waits for them, and re-layouts, key_slice(): lax.dynamic_slice_in_dim(all_values, begin, size, 0)  12 us
  transfers between devices with their start and end apart: 3, of which 3 were waited for; matrix products, arithmetic and copies ran while one was open for 3% of the time, Pallas kernels for 0%

profile of v1, /device:TPU:1, one launch (start us, length us, event | category | flops | bytes accessed | tf_op | source)
XLA Modules:
  0.0 318.4 jit_solution(3728979152250896261)
XLA Ops:
  7.2 0.7 broadcast_bitcast_fusion
  7.8 0.9 reshape.130
  9.3 0.9 fusion.33
  10.3 1.2 stack.3
  11.5 13.4 %all-to-all-start = ((bf16[16,128,256]{1,2,0:T(8,128)(2,1)}), bf16[16,128,256]{1,2,0:T(8,128)(2,1)S(1)}, u32[]{:S(2)}, u32[]{:S(2)}) async-start(bf16[16,128,256]{1,2,0:T(8,128)(2,1)} %stack.3), calls=%async_computation | async-start | bytes 2097152 | tf_op jit(solution)/shard_map/all_to_all | solution.py:61
  25.0 0.7 copy.120
  26.5 20.2 %all-to-all-done = bf16[16,128,256]{1,2,0:T(8,128)(2,1)S(1)} async-done(((bf16[16,128,256]{1,2,0:T(8,128)(2,1)}), bf16[16,128,256]{1,2,0:T(8,128)(2,1)S(1)}, u32[]{:S(2)}, u32[]{:S(2)}) %all-to-all-start) | async-done | bytes 1048608 | tf_op jit(solution)/shard_map/all_to_all | solution.py:61
  46.8 0.5 copy.119
  47.3 0.6 copy.125
  48.0 44.7 %all-gather.3.cloned.1.call-done = bf16[1,2048,256]{1,2,0:T(8,128)(2,1)} async-done(((bf16[1,128,256]{1,2,0:T(8,128)(2,1)}), bf16[1,2048,256]{1,2,0:T(8,128)(2,1)}) %all-gather.3.cloned.1.call-update) | async-done | bytes 1048592 | tf_op jit(solution)/shard_map/all_gather | solution.py:66
  92.7 7.0 %while.43 = (s32[]{:T(128)}, f32[2,128]{1,0:T(2,128)S(1)}, f32[2,128]{1,0:T(2,128)S(1)}, f32[2,128]{1,0:T(2,128)S(1)}, bf16[2048,256]{0,1:T(8,128)(2,1)S(1)}, /*...) while((s32[]{:T(128)}, f32[2,128]{1,0:T(2,128)S(1)}, ...), condition=%wide.region_6.0_spmd.clone, body=%wide.region_2.0_spmd.clone.sunk | while | flops 68028160 | bytes 3295418 | solution.py:95
  92.7 1.0 constant_dynamic-slice_fusion.10
  94.4 1.0 constant_dynamic-slice_fusion.10
  96.2 1.0 constant_dynamic-slice_fusion.10
  98.0 1.0 constant_dynamic-slice_fusion.10
  99.7 16.4 %while.42 = (s32[]{:T(128)}, bf16[4,512,512]{1,2,0:T(8,128)(2,1)}, s32[4]{0:T(128)S(1)}, bf16[2048,256]{0,1:T(8,128)(2,1)S(1)}, bf16[128,2,128]{0,2,1:T(8,128)(2...) while((s32[]{:T(128)}, bf16[4,512,512]{1,2,0:T(8,128)(2,1)}, ...), condition=%wide.region_11.12_spmd, body=%wide.region_10.0_spmd.sunk | while | flops 136183808 | bytes 4982983 | solution.py:118
  99.7 0.6 dynamic_slice.53
  101.0 1.0 constant_dynamic-slice_fusion.9
  102.3 0.5 fusion.88
  103.0 0.8 fusion.89
  103.8 0.6 dynamic_slice.53
  105.1 1.0 constant_dynamic-slice_fusion.9
  106.4 0.5 fusion.88
  107.1 0.9 fusion.89
  108.0 0.6 dynamic_slice.53
  109.2 1.0 constant_dynamic-slice_fusion.9
  110.5 0.5 fusion.88
  111.2 0.8 fusion.89
  112.0 0.6 dynamic_slice.53
  113.3 1.0 constant_dynamic-slice_fusion.9
  114.6 0.5 fusion.88
  115.3 0.9 fusion.89
  116.2 4.1 %copy.130 = bf16[4,512,512]{2,1,0:T(8,128)(2,1)} copy(bf16[4,512,512]{1,2,0:T(8,128)(2,1)} %get-tuple-element.336) | data formatting | bytes 4194304 | tf_op jit(solution)/shard_map/convert_element_type | solution.py:120
  120.4 7.3 %while.44 = (s32[]{:T(128)}, f32[128,2,128]{0,2,1:T(8,128)S(1)}, bf16[2048,256]{0,1:T(8,128)(2,1)S(1)}, bf16[128,2,128]{2,0,1:T(8,128)(2,1)S(1)}, f32[2,128]{1,0...) while((s32[]{:T(128)}, f32[128,2,128]{0,2,1:T(8,128)S(1)}, ...), condition=%wide.region_8.0_spmd.clone, body=%wide.region_7.0_spmd.clone.sunk | while | flops 101515264 | bytes 3279033 | solution.py:106
  120.4 1.0 constant_dynamic-slice_fusion.11
  121.7 0.5 fusion.105
  122.2 1.0 constant_dynamic-slice_fusion.11
  123.5 0.5 fusion.105
  124.0 1.0 constant_dynamic-slice_fusion.11
  125.3 0.5 fusion.105
  125.8 1.0 constant_dynamic-slice_fusion.11
  127.1 0.5 fusion.105
  127.9 0.7 copy.141
  128.6 82.5 %reduce-scatter.2.cloned.1.call-done = bf16[128,512]{1,0:T(8,128)(2,1)} async-done(((bf16[2048,512]{1,0:T(8,128)(2,1)}), bf16[128,512]{1,0:T(8,128)(2,1)}) %reduce-scatter.2.cloned.1.call-update) | async-done | bytes 131088 | tf_op jit(solution)/shard_map/reduce_scatter | solution.py:117
  211.2 1.5 slice_bitcast_fusion
  213.3 1.5 multiply_reduce_fusion
  214.9 96.2 %all-reduce = (f32[128]{0:T(128)S(1)}, f32[128]{0:T(128)S(1)}) all-reduce(f32[128]{0:T(128)S(1)} %get-tuple-element.541, f32[128]{0:T(128)S(1)} %bitcast_reduce_fusion), channel_id=1, replica_groups=mesh['ctx'=16,'tp'=8,'dp'=4] {'ctx','tp','dp'}, use_global_device_ids=true, to_apply=%region_15.16 | all-reduce | flops 256 | bytes 2048 | tf_op jit(solution)/shard_map/psum | solution.py:130
  311.1 0.5 broadcast_multiply_fusion.2
  (79 shorter events, 8.4 us)
Async XLA Ops:
  8.9 16.1 %copy-start.2 = (bf16[1,128,256]{2,1,0:T(8,128)(2,1)S(1)}, bf16[1,128,256]{2,1,0:T(8,128)(2,1)}, u32[]{:S(2)}) copy-start(bf16[1,128,256]{2,1,0:T(8,128)(2,1)} %param.14) | copy-start | bytes 196612
  9.0 16.9 %copy-start.3 = (bf16[1,128,256]{2,1,0:T(8,128)(2,1)S(1)}, bf16[1,128,256]{2,1,0:T(8,128)(2,1)}, u32[]{:S(2)}) copy-start(bf16[1,128,256]{2,1,0:T(8,128)(2,1)} %param.15) | copy-start | bytes 196612
  9.3 16.8 %copy-start.1 = (bf16[1,128,256]{2,1,0:T(8,128)(2,1)S(1)}, bf16[1,128,256]{2,1,0:T(8,128)(2,1)}, u32[]{:S(2)}) copy-start(bf16[1,128,256]{2,1,0:T(8,128)(2,1)} %param.12) | copy-start | bytes 196612
  10.2 16.1 %copy-start.4 = (f32[128]{0:T(128)S(1)}, f32[128]{0:T(128)}, u32[]{:S(2)}) copy-start(f32[128]{0:T(128)} %param.16) | copy-start | bytes 1540
  11.5 35.2 %all-to-all-start = ((bf16[16,128,256]{1,2,0:T(8,128)(2,1)}), bf16[16,128,256]{1,2,0:T(8,128)(2,1)S(1)}, u32[]{:S(2)}, u32[]{:S(2)}) async-start(bf16[16,128,256]{1,2,0:T(8,128)(2,1)} %stack.3), calls=%async_computation | async-start | bytes 2097152 | tf_op jit(solution)/shard_map/all_to_all | solution.py:61
  25.0 67.7 %all-gather.3.cloned.1.call-start = ((), (), s32[]{:S(2)}) async-start(), calls=%async_computation.3 | async-start | bytes 1114112 | tf_op jit(solution)/shard_map/all_gather | solution.py:66
  25.8 185.4 %reduce-scatter.2.cloned.1.call-start = ((), (), s32[]{:S(2)}) async-start(), calls=%async_computation.2 | async-start | bytes 2228224 | tf_op jit(solution)/shard_map/reduce_scatter | solution.py:117
  120.3 92.4 %copy-start.5 = (f32[128]{0:T(128)S(1)}, f32[128]{0:T(128)}, u32[]{:S(2)}) copy-start(f32[128]{0:T(128)} %param.17) | copy-start | bytes 1540
  120.4 93.0 %copy-start = (bf16[1,128,256]{2,1,0:T(8,128)(2,1)S(1)}, bf16[1,128,256]{2,1,0:T(8,128)(2,1)}, u32[]{:S(2)}) copy-start(bf16[1,128,256]{2,1,0:T(8,128)(2,1)} %param.13) | copy-start | bytes 196612
Sparse Core Ops, SparseCore 0:
  29.4 63.2 all-gather.2
  120.5 90.6 reduce-scatter.1
